TPU v7x, 32 devices: a whole 2x2x4 slice. The times are simulated.
32 devices in a mesh: tm: 2 (over x), grid: 16 (over z, y, core).
Axes of the slice: x: 2, y: 2, z: 4, core: 2. Of those that a mesh axis runs over, the one named last changes fastest.
Arguments:
- occupied_green: bfloat16 [2, 1024, 1024], P('tm', 'grid'), may hold values from -0.005859375 to 0.005859375
- empty_green: bfloat16 [2, 1024, 1024], P('tm', 'grid'), may hold values from -0.005859375 to 0.005859375
- basis: bfloat16 [12288, 1024], P('grid'), may hold values from -8 to 8
- time_weights: float32 [2, 2], replicated, may hold values from 0.25 to 1
Outputs:
- polarizability: float32 [2, 1024, 1024], P('tm', 'grid')
All inputs are finite; a program needn't handle non-finite values.
Results may differ from a plain program's by a relative error of at most 0.0012.
Values may be sent and summed in bfloat16 or wider, within the bound.
A program may use at most 128 MiB of HBM per device.

v0:
```python
import jax
import jax.numpy as jnp
from jax import lax
from jax.sharding import PartitionSpec as P

NR = 12288
NB = 1024


def weigh_times(time_weights, block_list, scale_factor):
    time_count = len(block_list)
    group_index = lax.axis_index("tm")
    weights_local = lax.dynamic_slice_in_dim(time_weights, group_index * time_count, time_count, 1)
    accum = weights_local[:, 0, None, None] * block_list[0][None]
    return scale_factor * accum


def step_size(piece_rows):
    return max((divisor for divisor in range(1, 2049) if piece_rows % divisor == 0))


def shards(occupied_green, empty_green, basis, time_weights):
    stacked = jnp.stack([occupied_green, empty_green])
    time_count = occupied_green.shape[0]
    coef_block = occupied_green.shape[1]
    row_total = basis.shape[0]
    scale_factor = 1.0 / NR

    def make_accumulate(combined_rows):

        def accumulate(running, basis_piece, first_row):
            piece_rows = basis_piece.shape[0]
            step_rows = step_size(piece_rows)

            def one_step(step_index, inner):
                basis_subpart = lax.dynamic_slice_in_dim(
                    basis_piece, step_index * step_rows, step_rows, 0
                )
                real_pair = jnp.einsum(
                    "qoa,ba->qob", combined_rows, basis_subpart, preferred_element_type=jnp.float32
                )
                product = (real_pair[0] * real_pair[1]).astype(jnp.bfloat16)
                return inner + jnp.dot(product, basis_subpart, preferred_element_type=jnp.float32)

            return lax.fori_loop(0, piece_rows // step_rows, one_step, running)

        return accumulate

    initial = jnp.zeros((time_count * row_total, NB), jnp.float32)
    projected = jnp.einsum(
        "sl,ftkl->ftsk",
        basis,
        lax.all_gather(stacked, "grid", axis=2, tiled=True),
        preferred_element_type=jnp.float32,
    ).astype(jnp.bfloat16)
    combined_rows = projected.reshape(2, time_count * row_total, NB)
    accumulate = make_accumulate(combined_rows)
    summed = accumulate(initial, lax.all_gather(basis, "grid", axis=0, tiled=True), jnp.int32(0))
    back_half = summed.astype(jnp.bfloat16).reshape(time_count, row_total, NB)
    coef_rows = lax.psum_scatter(
        jnp.einsum("tsk,sl->ktl", back_half, basis, preferred_element_type=jnp.float32).reshape(
            lax.axis_size("grid") * coef_block, time_count * NB
        ),
        "grid",
        scatter_dimension=0,
        tiled=True,
    ).reshape(coef_block, time_count, NB)
    block_list = [coef_rows[:, 0]]
    result = lax.psum_scatter(
        weigh_times(time_weights, block_list, scale_factor), "tm", scatter_dimension=0, tiled=True
    )
    return result


def solution(mesh):
    in_specs = (P("tm", "grid", None), P("tm", "grid", None), P("grid", None), P())
    out_specs = P("tm", "grid", None)
    return jax.shard_map(shards, mesh=mesh, in_specs=in_specs, out_specs=out_specs, check_vma=False)
```

profile of v0, /device:TPU:0, one launch (start us, length us, event | category | flops | bytes accessed | tf_op | source)
XLA Modules:
  0.0 431.6 jit_solution(16188916720244867342)
XLA Ops:
  6.5 0.0 copy-start
  6.5 0.0 all-gather.5.cloned.1.call-start
  6.5 1.7 pad_maximum_fusion
  8.2 0.0 all-gather.5.cloned.1.call-update
  8.3 0.0 all-gather.3.cloned.1.call-start
  8.3 0.7 all-gather.3.cloned.1.call-update
  9.0 0.0 reduce-scatter.3.cloned.1.call-start
  9.1 53.6 %all-gather.5.cloned.1.call-done = bf16[2,1,1024,1024]{3,2,0,1:T(8,128)(2,1)} async-done(((bf16[2,1,64,1024]{3,2,0,1:T(8,128)(2,1)}), bf16[2,1,1024,1024]{3,2,0,1:T(8,128)(2,1)}) %all-gather.5.cloned.1.call-update) | async-done | bytes 4194320 | tf_op jit(solution)/shard_map/all_gather | solution.py:53
  62.7 7.9 %convert_bitcast_fusion = bf16[2,768,1024]{1,2,0:T(8,128)(2,1)} fusion(bf16[2,1,1024,1024]{3,2,0,1:T(8,128)(2,1)} %all-gather.5.cloned.1.call-done, bf16[768,1024]{1,0:T(8,128)(2,1)} %param.8), kind=kOutput, calls=%fused_computation.13 | convolution fusion | flops 3222798336 | bytes 8912896 | tf_op jit(solution)/shard_map/sl,ftkl->ftsk/dot_general | solution.py:50
  70.5 3.2 copy.5
  73.8 117.6 %all-gather.3.cloned.1.call-done = bf16[12288,1024]{1,0:T(8,128)(2,1)} async-done(((bf16[768,1024]{1,0:T(8,128)(2,1)}), bf16[12288,1024]{1,0:T(8,128)(2,1)}) %all-gather.3.cloned.1.call-update) | async-done | bytes 25165840 | tf_op jit(solution)/shard_map/all_gather | solution.py:58
  191.3 138.8 %while.14 = (s32[]{:T(128)}, f32[768,1024]{1,0:T(8,128)}, bf16[12288,1024]{1,0:T(8,128)(2,1)}, bf16[2,768,1024]{2,1,0:T(8,128)(2,1)S(1)}, s32[]{:T(128)}, /*index=5*/s32[]{:T(128)}, s32[]{:T(128)}, s32[]{:T(128)}) while((s32[]{:T(128)}, f32[768,1024]{1,0:T(8,128)}, bf16[12288,1024]{1,0:T(8,128)(2,1)}, ...), condition=%wide.region_1.0_spmd.clone, body=%wide.region_0.0_spmd.clone.sunk | while | flops 9668395008 | bytes 42991772 | solution.py:45
  191.4 11.5 %convolution_bitcast_fusion.2 = f32[2,768,2048]{1,2,0:T(8,128)} fusion(bf16[2,768,1024]{2,1,0:T(8,128)(2,1)S(1)} %get-tuple-element.156, bf16[12288,1024]{1,0:T(8,128)(2,1)} %get-tuple-element.155, s32[]{:T(128)S(6)} %select_n.13), kind=kOutput, calls=%fused_computation.2.clone.1 | convolution fusion | flops 6442450944 | bytes 19922948 | tf_op jit(solution)/shard_map/while/body/eval_jaxpr/qoa,ba->qob/dot_general | solution.py:39
  202.9 10.9 %select_add_fusion.2 = f32[768,1024]{1,0:T(8,128)} fusion(f32[768,1024]{1,0:T(8,128)} %get-tuple-element.146, bf16[12288,1024]{1,0:T(8,128)(2,1)} %get-tuple-element.155, s32[]{:T(128)S(6)} %select_n.13, f32[2,768,2048]{1,2,0:T(8,128)} %convolution_bitcast_fusion.2, pred[]{:T(512)S(6)} %compare.3), kind=kOutput, calls=%fused_computation.8.clone.1 | convolution fusion | flops 3225944064 | bytes 23068676 | tf_op jit(solution)/shard_map/while/body/eval_jaxpr/dot_general | solution.py:43
  213.7 11.5 %convolution_bitcast_fusion.2 = f32[2,768,2048]{1,2,0:T(8,128)} fusion(bf16[2,768,1024]{2,1,0:T(8,128)(2,1)S(1)} %get-tuple-element.156, bf16[12288,1024]{1,0:T(8,128)(2,1)} %get-tuple-element.155, s32[]{:T(128)S(6)} %select_n.13), kind=kOutput, calls=%fused_computation.2.clone.1 | convolution fusion | flops 6442450944 | bytes 19922948 | tf_op jit(solution)/shard_map/while/body/eval_jaxpr/qoa,ba->qob/dot_general | solution.py:39
  225.2 11.8 %select_add_fusion.2 = f32[768,1024]{1,0:T(8,128)} fusion(f32[768,1024]{1,0:T(8,128)} %get-tuple-element.146, bf16[12288,1024]{1,0:T(8,128)(2,1)} %get-tuple-element.155, s32[]{:T(128)S(6)} %select_n.13, f32[2,768,2048]{1,2,0:T(8,128)} %convolution_bitcast_fusion.2, pred[]{:T(512)S(6)} %compare.3), kind=kOutput, calls=%fused_computation.8.clone.1 | convolution fusion | flops 3225944064 | bytes 23068676 | tf_op jit(solution)/shard_map/while/body/eval_jaxpr/dot_general | solution.py:43
  237.0 11.5 %convolution_bitcast_fusion.2 = f32[2,768,2048]{1,2,0:T(8,128)} fusion(bf16[2,768,1024]{2,1,0:T(8,128)(2,1)S(1)} %get-tuple-element.156, bf16[12288,1024]{1,0:T(8,128)(2,1)} %get-tuple-element.155, s32[]{:T(128)S(6)} %select_n.13), kind=kOutput, calls=%fused_computation.2.clone.1 | convolution fusion | flops 6442450944 | bytes 19922948 | tf_op jit(solution)/shard_map/while/body/eval_jaxpr/qoa,ba->qob/dot_general | solution.py:39
  248.5 11.8 %select_add_fusion.2 = f32[768,1024]{1,0:T(8,128)} fusion(f32[768,1024]{1,0:T(8,128)} %get-tuple-element.146, bf16[12288,1024]{1,0:T(8,128)(2,1)} %get-tuple-element.155, s32[]{:T(128)S(6)} %select_n.13, f32[2,768,2048]{1,2,0:T(8,128)} %convolution_bitcast_fusion.2, pred[]{:T(512)S(6)} %compare.3), kind=kOutput, calls=%fused_computation.8.clone.1 | convolution fusion | flops 3225944064 | bytes 23068676 | tf_op jit(solution)/shard_map/while/body/eval_jaxpr/dot_general | solution.py:43
  260.3 11.5 %convolution_bitcast_fusion.2 = f32[2,768,2048]{1,2,0:T(8,128)} fusion(bf16[2,768,1024]{2,1,0:T(8,128)(2,1)S(1)} %get-tuple-element.156, bf16[12288,1024]{1,0:T(8,128)(2,1)} %get-tuple-element.155, s32[]{:T(128)S(6)} %select_n.13), kind=kOutput, calls=%fused_computation.2.clone.1 | convolution fusion | flops 6442450944 | bytes 19922948 | tf_op jit(solution)/shard_map/while/body/eval_jaxpr/qoa,ba->qob/dot_general | solution.py:39
  271.8 11.8 %select_add_fusion.2 = f32[768,1024]{1,0:T(8,128)} fusion(f32[768,1024]{1,0:T(8,128)} %get-tuple-element.146, bf16[12288,1024]{1,0:T(8,128)(2,1)} %get-tuple-element.155, s32[]{:T(128)S(6)} %select_n.13, f32[2,768,2048]{1,2,0:T(8,128)} %convolution_bitcast_fusion.2, pred[]{:T(512)S(6)} %compare.3), kind=kOutput, calls=%fused_computation.8.clone.1 | convolution fusion | flops 3225944064 | bytes 23068676 | tf_op jit(solution)/shard_map/while/body/eval_jaxpr/dot_general | solution.py:43
  283.6 11.5 %convolution_bitcast_fusion.2 = f32[2,768,2048]{1,2,0:T(8,128)} fusion(bf16[2,768,1024]{2,1,0:T(8,128)(2,1)S(1)} %get-tuple-element.156, bf16[12288,1024]{1,0:T(8,128)(2,1)} %get-tuple-element.155, s32[]{:T(128)S(6)} %select_n.13), kind=kOutput, calls=%fused_computation.2.clone.1 | convolution fusion | flops 6442450944 | bytes 19922948 | tf_op jit(solution)/shard_map/while/body/eval_jaxpr/qoa,ba->qob/dot_general | solution.py:39
  295.1 11.8 %select_add_fusion.2 = f32[768,1024]{1,0:T(8,128)} fusion(f32[768,1024]{1,0:T(8,128)} %get-tuple-element.146, bf16[12288,1024]{1,0:T(8,128)(2,1)} %get-tuple-element.155, s32[]{:T(128)S(6)} %select_n.13, f32[2,768,2048]{1,2,0:T(8,128)} %convolution_bitcast_fusion.2, pred[]{:T(512)S(6)} %compare.3), kind=kOutput, calls=%fused_computation.8.clone.1 | convolution fusion | flops 3225944064 | bytes 23068676 | tf_op jit(solution)/shard_map/while/body/eval_jaxpr/dot_general | solution.py:43
  306.9 11.5 %convolution_bitcast_fusion.2 = f32[2,768,2048]{1,2,0:T(8,128)} fusion(bf16[2,768,1024]{2,1,0:T(8,128)(2,1)S(1)} %get-tuple-element.156, bf16[12288,1024]{1,0:T(8,128)(2,1)} %get-tuple-element.155, s32[]{:T(128)S(6)} %select_n.13), kind=kOutput, calls=%fused_computation.2.clone.1 | convolution fusion | flops 6442450944 | bytes 19922948 | tf_op jit(solution)/shard_map/while/body/eval_jaxpr/qoa,ba->qob/dot_general | solution.py:39
  318.4 11.8 %select_add_fusion.2 = f32[768,1024]{1,0:T(8,128)} fusion(f32[768,1024]{1,0:T(8,128)} %get-tuple-element.146, bf16[12288,1024]{1,0:T(8,128)(2,1)} %get-tuple-element.155, s32[]{:T(128)S(6)} %select_n.13, f32[2,768,2048]{1,2,0:T(8,128)} %convolution_bitcast_fusion.2, pred[]{:T(512)S(6)} %compare.3), kind=kOutput, calls=%fused_computation.8.clone.1 | convolution fusion | flops 3225944064 | bytes 23068676 | tf_op jit(solution)/shard_map/while/body/eval_jaxpr/dot_general | solution.py:43
  330.2 6.1 %fusion.18 = f32[1024,1024]{1,0:T(8,128)} fusion(bf16[768,1024]{1,0:T(8,128)(2,1)} %param.8, f32[768,1024]{1,0:T(8,128)} %get-tuple-element.84), kind=kOutput, calls=%fused_computation.15 | convolution fusion | flops 1611399168 | bytes 8912896 | tf_op jit(solution)/shard_map/tsk,sl->ktl/dot_general | solution.py:61
  336.3 0.0 reduce-scatter.3.cloned.1.call-update
  336.3 0.0 reduce-scatter.5.cloned.1.call-start
  336.4 0.2 dynamic-slice_reduce_fusion
  336.6 72.7 %reduce-scatter.3.cloned.1.call-done = f32[64,1024]{1,0:T(8,128)} async-done(((f32[1024,1024]{1,0:T(8,128)}), f32[64,1024]{1,0:T(8,128)}) %reduce-scatter.3.cloned.1.call-update) | async-done | bytes 262160 | tf_op jit(solution)/shard_map/reduce_scatter | solution.py:60
  409.2 1.9 multiply_multiply_fusion
  411.1 0.0 reduce-scatter.5.cloned.1.call-update
  411.1 13.9 %reduce-scatter.5.cloned.1.call-done = f32[1,64,1024]{2,1,0:T(8,128)} async-done(((f32[2,64,1024]{2,1,0:T(8,128)}), f32[1,64,1024]{2,1,0:T(8,128)}) %reduce-scatter.5.cloned.1.call-update) | async-done | bytes 262160 | tf_op jit(solution)/shard_map/reduce_scatter | solution.py:69
  (2 shorter events, 0.0 us)
Async XLA Ops:
  6.5 329.8 %copy-start = (f32[2,2]{1,0:T(2,128)S(1)}, f32[2,2]{1,0:T(2,128)}, u32[]{:S(2)}) copy-start(f32[2,2]{1,0:T(2,128)} %param.9) | copy-start | bytes 52
  6.5 56.1 %all-gather.5.cloned.1.call-start = ((), (), s32[]{:S(2)}) async-start(), calls=%async_computation.3 | async-start | bytes 4456448 | tf_op jit(solution)/shard_map/all_gather | solution.py:53
  8.3 183.1 %all-gather.3.cloned.1.call-start = ((), (), s32[]{:S(2)}) async-start(), calls=%async_computation.2 | async-start | bytes 26738688 | tf_op jit(solution)/shard_map/all_gather | solution.py:58
  9.0 400.2 %reduce-scatter.3.cloned.1.call-start = ((), (), s32[]{:S(2)}) async-start(), calls=%async_computation.4 | async-start | bytes 4456448 | tf_op jit(solution)/shard_map/reduce_scatter | solution.py:60
  336.3 88.8 %reduce-scatter.5.cloned.1.call-start = ((), (), s32[]{:S(2)}) async-start(), calls=%async_computation.5 | async-start | bytes 786432 | tf_op jit(solution)/shard_map/reduce_scatter | solution.py:69
Sparse Core Ops, SparseCore 0:
  9.5 53.1 all-gather.4
  64.3 127.0 all-gather.2
  336.4 72.7 reduce-scatter.2
  411.3 13.6 reduce-scatter.4
where the time goes:
time: 432 us
  waiting for transfers between devices  259 us (60%)
  matrix products  153 us (35%)
  between operations  13.2 us (3%)
    all_gather x1, waiting for transfers between devices, shards(): lax.all_gather(basis, 'grid', axis=0, tiled=True)  118 us
    reduce_scatter x1, waiting for transfers between devices, shards(): lax.psum_scatter(jnp.einsum('tsk,sl->ktl', back_half, basis, preferred_el...  72.7 us
    dot_general x6, matrix products, one_step(): jnp.dot(product, basis_subpart, preferred_element_type=jnp.float32)  69.8 us
    dot_general x6, matrix products, one_step(): jnp.einsum('qoa,ba->qob', combined_rows, basis_subpart, preferred_element...  69 us
    all_gather x1, waiting for transfers between devices, shards(): lax.all_gather(stacked, 'grid', axis=2, tiled=True)  53.6 us
    reduce_scatter x1, waiting for transfers between devices, shards(): lax.psum_scatter(weigh_times(time_weights, block_list, scale_factor), 'tm...  13.9 us
  transfers between devices with their start and end apart: 4, of which 4 were waited for; matrix products, arithmetic and copies ran while one was open for 3% of the time, Pallas kernels for 0%

commit v1 on v0

--- a/solution.py
+++ b/solution.py
@@ -5,6 +5,28 @@
 
 NR = 12288
 NB = 1024
+
+
+def laid_out(blocks, dim):
+    shape = list(blocks.shape[1:])
+    shape[dim] *= blocks.shape[0]
+    return jnp.moveaxis(blocks, 0, dim).reshape(shape)
+
+
+def collect(x, axis, dim):
+    devices = lax.axis_size(axis)
+    pairs = [(i, (i + 1) % devices) for i in range(devices)]
+    back = [(b, a) for a, b in pairs]
+    lower, upper = ([], [])
+    for turn in range(devices - 1):
+        if turn % 2 == 0:
+            lower.append(lax.ppermute(lower[-1] if lower else x, axis, pairs))
+        else:
+            upper.append(lax.ppermute(upper[-1] if upper else x, axis, back))
+    parts = jnp.stack([*lower[::-1], x, *upper])
+    shift = lax.axis_index(axis) - len(lower)
+    parts = parts[(jnp.arange(devices) - shift) % devices]
+    return laid_out(parts, dim)
 
 
 def weigh_times(time_weights, block_list, scale_factor):
@@ -55,7 +77,7 @@
     ).astype(jnp.bfloat16)
     combined_rows = projected.reshape(2, time_count * row_total, NB)
     accumulate = make_accumulate(combined_rows)
-    summed = accumulate(initial, lax.all_gather(basis, "grid", axis=0, tiled=True), jnp.int32(0))
+    summed = accumulate(initial, collect(basis, "grid", 0), jnp.int32(0))
     back_half = summed.astype(jnp.bfloat16).reshape(time_count, row_total, NB)
     coef_rows = lax.psum_scatter(
         jnp.einsum("tsk,sl->ktl", back_half, basis, preferred_element_type=jnp.float32).reshape(

time: 432 us -> 587 us (1.36)
  starting transfers between devices: 0.12 us -> 177 us
  waiting for transfers between devices: 259 us -> 185 us
  local copies, waits for them, and re-layouts: 3.4 us -> 54.3 us
    ppermute x0 -> x15, starting transfers between devices: none -> 177 us  [the longest x8 173 us: collect(): lower.append(lax.ppermute(lower[-1] if lower else x, axis, pairs))]
    all_gather x1 -> x0, waiting for transfers between devices: 118 us -> none  [shards(): lax.all_gather(basis, 'grid', axis=0, tiled=True)]
    ppermute x0 -> x15, waiting for transfers between devices: none -> 71.8 us  [the longest x8 71.8 us: collect(): lower.append(lax.ppermute(lower[-1] if lower else x, axis, pairs))]
    all_gather x1, waiting for transfers between devices: 53.6 us -> 0.02 us  [shards(): lax.all_gather(stacked, 'grid', axis=2, tiled=True)]
    unnamed x3 -> x56, local copies, waits for them, and re-layouts: 3.21 us -> 34.6 us
    reduce_scatter x1, waiting for transfers between devices: 72.7 us -> 99.4 us  [shards(): lax.psum_scatter(jnp.einsum('tsk,sl->ktl', back_half, basis, preferred_el...]
    gather x0 -> x1, local copies, waits for them, and re-layouts: none -> 18.2 us  [collect(): parts = parts[(jnp.arange(devices) - shift) % devices]]
  transfers between devices with their start and end apart: 4 -> 18, of which waited for: 4 -> 9; matrix products, arithmetic and copies ran while one was open for 3% -> 7% of each run, Pallas kernels for 0% -> 0%
where the time goes in v1:
time: 587 us
  waiting for transfers between devices  185 us (32%)
  starting transfers between devices  177 us (30%)
  matrix products  153 us (26%)
  local copies, waits for them, and re-layouts  54.3 us (9%)
  between operations  13.3 us (2%)
    ppermute x8, starting transfers between devices, collect(): lower.append(lax.ppermute(lower[-1] if lower else x, axis, pairs))  173 us
    reduce_scatter x1, waiting for transfers between devices, shards(): lax.psum_scatter(jnp.einsum('tsk,sl->ktl', back_half, basis, preferred_el...  99.4 us
    ppermute x8, waiting for transfers between devices, collect(): lower.append(lax.ppermute(lower[-1] if lower else x, axis, pairs))  71.8 us
    dot_general x6, matrix products, one_step(): jnp.dot(product, basis_subpart, preferred_element_type=jnp.float32)  69.9 us
    dot_general x6, matrix products, one_step(): jnp.einsum('qoa,ba->qob', combined_rows, basis_subpart, preferred_element...  68.8 us
    unnamed x56, local copies, waits for them, and re-layouts  34.6 us
    gather x1, local copies, waits for them, and re-layouts, collect(): parts = parts[(jnp.arange(devices) - shift) % devices]  18.2 us
    reduce_scatter x1, waiting for transfers between devices, shards(): lax.psum_scatter(weigh_times(time_weights, block_list, scale_factor), 'tm...  14.1 us
  transfers between devices with their start and end apart: 18, of which 9 were waited for; matrix products, arithmetic and copies ran while one was open for 7% of the time, Pallas kernels for 0%

profile of v1, /device:TPU:0, one launch (start us, length us, event | category | flops | bytes accessed | tf_op | source)
XLA Modules:
  0.0 586.8 jit_solution(5886556723408446443)
XLA Ops:
  7.0 23.3 %collective-permute-done = bf16[768,1024]{1,0:T(8,128)(2,1)S(1)} collective-permute-done((bf16[768,1024]{1,0:T(8,128)(2,1)}, bf16[768,1024]{1,0:T(8,128)(2,1)S(1)}, u32[]{:S(2)}, u32[]{:S(2)}) %collective-permute-start) | collective-permute-done | bytes 1572896 | tf_op jit(solution)/shard_map/ppermute | solution.py:23
  31.5 4.4 collective-permute-start.8
  35.9 18.2 %collective-permute-done.1 = bf16[768,1024]{1,0:T(8,128)(2,1)S(1)} collective-permute-done((bf16[768,1024]{1,0:T(8,128)(2,1)S(1)}, bf16[768,1024]{1,0:T(8,128)(2,1)S(1)}, u32[]{:S(2)}, u32[]{:S(2)}) %collective-permute-start.1) | collective-permute-done | bytes 1572896 | tf_op jit(solution)/shard_map/ppermute | solution.py:23
  54.1 11.0 %collective-permute-start.2 = (bf16[768,1024]{1,0:T(8,128)(2,1)S(1)}, bf16[768,1024]{1,0:T(8,128)(2,1)}, u32[]{:S(2)}, u32[]{:S(2)}) collective-permute-start(bf16[768,1024]{1,0:T(8,128)(2,1)S(1)} %collective-permute-done.1), channel_id=1, source_target_pairs={{0,1},{1,2},{2,3},{3,4},{4,5},{5,6},{6,7},{7,8},{8,9},{9,10},{10,1... | collective-permute-start | bytes 4718600 | tf_op jit(solution)/shard_map/ppermute | solution.py:23
  66.9 9.9 %collective-permute-done.2 = bf16[768,1024]{1,0:T(8,128)(2,1)} collective-permute-done((bf16[768,1024]{1,0:T(8,128)(2,1)S(1)}, bf16[768,1024]{1,0:T(8,128)(2,1)}, u32[]{:S(2)}, u32[]{:S(2)}) %collective-permute-start.2) | collective-permute-done | bytes 1572896 | tf_op jit(solution)/shard_map/ppermute | solution.py:23
  76.9 27.7 %collective-permute-start.3 = (bf16[768,1024]{1,0:T(8,128)(2,1)}, bf16[768,1024]{1,0:T(8,128)(2,1)S(1)}, u32[]{:S(2)}, u32[]{:S(2)}) collective-permute-start(bf16[768,1024]{1,0:T(8,128)(2,1)} %collective-permute-done.2), channel_id=1, source_target_pairs={{0,1},{1,2},{2,3},{3,4},{4,5},{5,6},{6,7},{7,8},{8,9},{9,10},{10,1... | collective-permute-start | bytes 4718600 | tf_op jit(solution)/shard_map/ppermute | solution.py:23
  105.7 5.6 collective-permute-done.3
  111.3 41.6 %collective-permute-start.4 = (bf16[768,1024]{1,0:T(8,128)(2,1)S(1)}, bf16[768,1024]{1,0:T(8,128)(2,1)S(1)}, u32[]{:S(2)}, u32[]{:S(2)}) collective-permute-start(bf16[768,1024]{1,0:T(8,128)(2,1)S(1)} %collective-permute-done.3), channel_id=1, source_target_pairs={{0,1},{1,2},{2,3},{3,4},{4,5},{5,6},{6,7},{7,8},{8,9},{9,10},{10,1... | collective-permute-start | bytes 4718600 | tf_op jit(solution)/shard_map/ppermute | solution.py:23
  154.1 9.7 %collective-permute-done.4 = bf16[768,1024]{1,0:T(8,128)(2,1)S(1)} collective-permute-done((bf16[768,1024]{1,0:T(8,128)(2,1)S(1)}, bf16[768,1024]{1,0:T(8,128)(2,1)S(1)}, u32[]{:S(2)}, u32[]{:S(2)}) %collective-permute-start.4) | collective-permute-done | bytes 1572896 | tf_op jit(solution)/shard_map/ppermute | solution.py:23
  163.8 25.7 %collective-permute-start.5 = (bf16[768,1024]{1,0:T(8,128)(2,1)S(1)}, bf16[768,1024]{1,0:T(8,128)(2,1)S(1)}, u32[]{:S(2)}, u32[]{:S(2)}) collective-permute-start(bf16[768,1024]{1,0:T(8,128)(2,1)S(1)} %collective-permute-done.4), channel_id=1, source_target_pairs={{0,1},{1,2},{2,3},{3,4},{4,5},{5,6},{6,7},{7,8},{8,9},{9,10},{10,1... | collective-permute-start | bytes 4718600 | tf_op jit(solution)/shard_map/ppermute | solution.py:23
  192.6 33.7 %collective-permute-start.6 = (bf16[768,1024]{1,0:T(8,128)(2,1)S(1)}, bf16[768,1024]{1,0:T(8,128)(2,1)}, u32[]{:S(2)}, u32[]{:S(2)}) collective-permute-start(bf16[768,1024]{1,0:T(8,128)(2,1)S(1)} %collective-permute-done.5), channel_id=1, source_target_pairs={{0,1},{1,2},{2,3},{3,4},{4,5},{5,6},{6,7},{7,8},{8,9},{9,10},{10,1... | collective-permute-start | bytes 4718600 | tf_op jit(solution)/shard_map/ppermute | solution.py:23
  226.2 3.1 collective-permute-done.6
  229.4 32.5 %collective-permute-start.7 = (bf16[768,1024]{1,0:T(8,128)(2,1)}, bf16[768,1024]{1,0:T(8,128)(2,1)}, u32[]{:S(2)}, u32[]{:S(2)}) collective-permute-start(bf16[768,1024]{1,0:T(8,128)(2,1)} %collective-permute-done.6), channel_id=1, source_target_pairs={{0,1},{1,2},{2,3},{3,4},{4,5},{5,6},{6,7},{7,8},{8,9},{9,10},{10,1... | collective-permute-start | bytes 4718600 | tf_op jit(solution)/shard_map/ppermute | solution.py:23
  262.0 7.9 %convert_bitcast_fusion = bf16[2,768,1024]{1,2,0:T(8,128)(2,1)} fusion(bf16[2,1,1024,1024]{3,2,0,1:T(8,128)(2,1)} %all-gather.2.cloned.1.call-done, bf16[768,1024]{1,0:T(8,128)(2,1)} %param.8), kind=kOutput, calls=%fused_computation.14 | convolution fusion | flops 3222798336 | bytes 8912896 | tf_op jit(solution)/shard_map/sl,ftkl->ftsk/dot_general | solution.py:72
  269.9 3.2 copy.5
  301.5 18.2 %gather_fusion = bf16[16,768,1024]{2,1,0:T(8,128)(2,1)} fusion(bf16[16,768,1024]{2,1,0:T(8,128)(2,1)} %bitcast_dynamic-update-slice_fusion, s32[1024]{0:T(1024)S(1)} %pad_clamp_fusion), kind=kCustom, calls=%fused_computation | custom fusion | bytes 50331712 | tf_op jit(solution)/shard_map/gather | solution.py:28
  319.8 138.7 %while.14 = (s32[]{:T(128)}, f32[768,1024]{1,0:T(8,128)}, bf16[12288,1024]{1,0:T(8,128)(2,1)}, bf16[2,768,1024]{2,1,0:T(8,128)(2,1)S(1)}, s32[]{:T(128)}, /*index=5*/s32[]{:T(128)}, s32[]{:T(128)}, s32[]{:T(128)}) while((s32[]{:T(128)}, f32[768,1024]{1,0:T(8,128)}, bf16[12288,1024]{1,0:T(8,128)(2,1)}, ...), condition=%wide.region_1.2_spmd.clone, body=%wide.region_0.1_spmd.clone.sunk | while | flops 9668395008 | bytes 42991764 | solution.py:67
  319.8 11.5 %convolution_bitcast_fusion.2 = f32[2,768,2048]{1,2,0:T(8,128)} fusion(bf16[2,768,1024]{2,1,0:T(8,128)(2,1)S(1)} %get-tuple-element.156, bf16[12288,1024]{1,0:T(8,128)(2,1)} %get-tuple-element.155, s32[]{:T(128)S(6)} %select_n.47), kind=kOutput, calls=%fused_computation.3.clone.1 | convolution fusion | flops 6442450944 | bytes 19922948 | tf_op jit(solution)/shard_map/while/body/eval_jaxpr/qoa,ba->qob/dot_general | solution.py:61
  331.2 10.9 %select_add_fusion.2 = f32[768,1024]{1,0:T(8,128)} fusion(f32[768,1024]{1,0:T(8,128)} %get-tuple-element.146, bf16[12288,1024]{1,0:T(8,128)(2,1)} %get-tuple-element.155, s32[]{:T(128)S(6)} %select_n.47, f32[2,768,2048]{1,2,0:T(8,128)} %convolution_bitcast_fusion.2, pred[]{:T(512)S(6)} %compare.10), kind=kOutput, calls=%fused_computation.9.clone.1 | convolution fusion | flops 3225944064 | bytes 23068676 | tf_op jit(solution)/shard_map/while/body/eval_jaxpr/dot_general | solution.py:65
  342.2 11.5 %convolution_bitcast_fusion.2 = f32[2,768,2048]{1,2,0:T(8,128)} fusion(bf16[2,768,1024]{2,1,0:T(8,128)(2,1)S(1)} %get-tuple-element.156, bf16[12288,1024]{1,0:T(8,128)(2,1)} %get-tuple-element.155, s32[]{:T(128)S(6)} %select_n.47), kind=kOutput, calls=%fused_computation.3.clone.1 | convolution fusion | flops 6442450944 | bytes 19922948 | tf_op jit(solution)/shard_map/while/body/eval_jaxpr/qoa,ba->qob/dot_general | solution.py:61
  353.6 11.8 %select_add_fusion.2 = f32[768,1024]{1,0:T(8,128)} fusion(f32[768,1024]{1,0:T(8,128)} %get-tuple-element.146, bf16[12288,1024]{1,0:T(8,128)(2,1)} %get-tuple-element.155, s32[]{:T(128)S(6)} %select_n.47, f32[2,768,2048]{1,2,0:T(8,128)} %convolution_bitcast_fusion.2, pred[]{:T(512)S(6)} %compare.10), kind=kOutput, calls=%fused_computation.9.clone.1 | convolution fusion | flops 3225944064 | bytes 23068676 | tf_op jit(solution)/shard_map/while/body/eval_jaxpr/dot_general | solution.py:65
  365.4 11.5 %convolution_bitcast_fusion.2 = f32[2,768,2048]{1,2,0:T(8,128)} fusion(bf16[2,768,1024]{2,1,0:T(8,128)(2,1)S(1)} %get-tuple-element.156, bf16[12288,1024]{1,0:T(8,128)(2,1)} %get-tuple-element.155, s32[]{:T(128)S(6)} %select_n.47), kind=kOutput, calls=%fused_computation.3.clone.1 | convolution fusion | flops 6442450944 | bytes 19922948 | tf_op jit(solution)/shard_map/while/body/eval_jaxpr/qoa,ba->qob/dot_general | solution.py:61
  376.9 11.8 %select_add_fusion.2 = f32[768,1024]{1,0:T(8,128)} fusion(f32[768,1024]{1,0:T(8,128)} %get-tuple-element.146, bf16[12288,1024]{1,0:T(8,128)(2,1)} %get-tuple-element.155, s32[]{:T(128)S(6)} %select_n.47, f32[2,768,2048]{1,2,0:T(8,128)} %convolution_bitcast_fusion.2, pred[]{:T(512)S(6)} %compare.10), kind=kOutput, calls=%fused_computation.9.clone.1 | convolution fusion | flops 3225944064 | bytes 23068676 | tf_op jit(solution)/shard_map/while/body/eval_jaxpr/dot_general | solution.py:65
  388.7 11.5 %convolution_bitcast_fusion.2 = f32[2,768,2048]{1,2,0:T(8,128)} fusion(bf16[2,768,1024]{2,1,0:T(8,128)(2,1)S(1)} %get-tuple-element.156, bf16[12288,1024]{1,0:T(8,128)(2,1)} %get-tuple-element.155, s32[]{:T(128)S(6)} %select_n.47), kind=kOutput, calls=%fused_computation.3.clone.1 | convolution fusion | flops 6442450944 | bytes 19922948 | tf_op jit(solution)/shard_map/while/body/eval_jaxpr/qoa,ba->qob/dot_general | solution.py:61
  400.2 11.8 %select_add_fusion.2 = f32[768,1024]{1,0:T(8,128)} fusion(f32[768,1024]{1,0:T(8,128)} %get-tuple-element.146, bf16[12288,1024]{1,0:T(8,128)(2,1)} %get-tuple-element.155, s32[]{:T(128)S(6)} %select_n.47, f32[2,768,2048]{1,2,0:T(8,128)} %convolution_bitcast_fusion.2, pred[]{:T(512)S(6)} %compare.10), kind=kOutput, calls=%fused_computation.9.clone.1 | convolution fusion | flops 3225944064 | bytes 23068676 | tf_op jit(solution)/shard_map/while/body/eval_jaxpr/dot_general | solution.py:65
  412.0 11.5 %convolution_bitcast_fusion.2 = f32[2,768,2048]{1,2,0:T(8,128)} fusion(bf16[2,768,1024]{2,1,0:T(8,128)(2,1)S(1)} %get-tuple-element.156, bf16[12288,1024]{1,0:T(8,128)(2,1)} %get-tuple-element.155, s32[]{:T(128)S(6)} %select_n.47), kind=kOutput, calls=%fused_computation.3.clone.1 | convolution fusion | flops 6442450944 | bytes 19922948 | tf_op jit(solution)/shard_map/while/body/eval_jaxpr/qoa,ba->qob/dot_general | solution.py:61
  423.4 11.8 %select_add_fusion.2 = f32[768,1024]{1,0:T(8,128)} fusion(f32[768,1024]{1,0:T(8,128)} %get-tuple-element.146, bf16[12288,1024]{1,0:T(8,128)(2,1)} %get-tuple-element.155, s32[]{:T(128)S(6)} %select_n.47, f32[2,768,2048]{1,2,0:T(8,128)} %convolution_bitcast_fusion.2, pred[]{:T(512)S(6)} %compare.10), kind=kOutput, calls=%fused_computation.9.clone.1 | convolution fusion | flops 3225944064 | bytes 23068676 | tf_op jit(solution)/shard_map/while/body/eval_jaxpr/dot_general | solution.py:65
  435.2 11.5 %convolution_bitcast_fusion.2 = f32[2,768,2048]{1,2,0:T(8,128)} fusion(bf16[2,768,1024]{2,1,0:T(8,128)(2,1)S(1)} %get-tuple-element.156, bf16[12288,1024]{1,0:T(8,128)(2,1)} %get-tuple-element.155, s32[]{:T(128)S(6)} %select_n.47), kind=kOutput, calls=%fused_computation.3.clone.1 | convolution fusion | flops 6442450944 | bytes 19922948 | tf_op jit(solution)/shard_map/while/body/eval_jaxpr/qoa,ba->qob/dot_general | solution.py:61
  446.7 11.8 %select_add_fusion.2 = f32[768,1024]{1,0:T(8,128)} fusion(f32[768,1024]{1,0:T(8,128)} %get-tuple-element.146, bf16[12288,1024]{1,0:T(8,128)(2,1)} %get-tuple-element.155, s32[]{:T(128)S(6)} %select_n.47, f32[2,768,2048]{1,2,0:T(8,128)} %convolution_bitcast_fusion.2, pred[]{:T(512)S(6)} %compare.10), kind=kOutput, calls=%fused_computation.9.clone.1 | convolution fusion | flops 3225944064 | bytes 23068676 | tf_op jit(solution)/shard_map/while/body/eval_jaxpr/dot_general | solution.py:65
  458.5 6.2 %fusion.18 = f32[1024,1024]{1,0:T(8,128)} fusion(bf16[768,1024]{1,0:T(8,128)(2,1)} %param.8, f32[768,1024]{1,0:T(8,128)} %get-tuple-element.84), kind=kOutput, calls=%fused_computation.32 | convolution fusion | flops 1611399168 | bytes 8912896 | tf_op jit(solution)/shard_map/tsk,sl->ktl/dot_general | solution.py:83
  464.9 99.4 %reduce-scatter.3.cloned.1.call-done = f32[64,1024]{1,0:T(8,128)} async-done(((f32[1024,1024]{1,0:T(8,128)}), f32[64,1024]{1,0:T(8,128)}) %reduce-scatter.3.cloned.1.call-update) | async-done | bytes 262160 | tf_op jit(solution)/shard_map/reduce_scatter | solution.py:82
  566.2 14.1 %reduce-scatter.5.cloned.1.call-done = f32[1,64,1024]{2,1,0:T(8,128)} async-done(((f32[2,64,1024]{2,1,0:T(8,128)}), f32[1,64,1024]{2,1,0:T(8,128)}) %reduce-scatter.5.cloned.1.call-update) | async-done | bytes 262160 | tf_op jit(solution)/shard_map/reduce_scatter | solution.py:91
  (86 shorter events, 39.3 us)
Async XLA Ops:
  6.5 458.2 %copy-start = (f32[2,2]{1,0:T(2,128)S(1)}, f32[2,2]{1,0:T(2,128)}, u32[]{:S(2)}) copy-start(f32[2,2]{1,0:T(2,128)} %param.9) | copy-start | bytes 52
  6.5 255.4 %all-gather.2.cloned.1.call-start = ((), (), s32[]{:S(2)}) async-start(), calls=%async_computation.2 | async-start | bytes 4456448 | tf_op jit(solution)/shard_map/all_gather | solution.py:75
  6.5 23.8 %collective-permute-start = (bf16[768,1024]{1,0:T(8,128)(2,1)}, bf16[768,1024]{1,0:T(8,128)(2,1)S(1)}, u32[]{:S(2)}, u32[]{:S(2)}) collective-permute-start(bf16[768,1024]{1,0:T(8,128)(2,1)} %param.8), channel_id=1, source_target_pairs={{0,1},{1,2},{2,3},{3,4},{4,5},{5,6},{6,7},{7,8},{8,9},{9,10},{10,1... | collective-permute-start | bytes 4718600 | tf_op jit(solution)/shard_map/ppermute | solution.py:23
  31.5 22.6 %collective-permute-start.1 = (bf16[768,1024]{1,0:T(8,128)(2,1)S(1)}, bf16[768,1024]{1,0:T(8,128)(2,1)S(1)}, u32[]{:S(2)}, u32[]{:S(2)}) collective-permute-start(bf16[768,1024]{1,0:T(8,128)(2,1)S(1)} %collective-permute-done), channel_id=1, source_target_pairs={{0,1},{1,2},{2,3},{3,4},{4,5},{5,6},{6,7},{7,8},{8,9},{9,10},{10,1... | collective-permute-start | bytes 4718600 | tf_op jit(solution)/shard_map/ppermute | solution.py:23
  31.5 35.4 %collective-permute-start.8 = (bf16[768,1024]{1,0:T(8,128)(2,1)}, bf16[768,1024]{1,0:T(8,128)(2,1)S(1)}, u32[]{:S(2)}, u32[]{:S(2)}) collective-permute-start(bf16[768,1024]{1,0:T(8,128)(2,1)} %param.8), channel_id=1, source_target_pairs={{1,0},{2,1},{3,2},{4,3},{5,4},{6,5},{7,6},{8,7},{9,8},{10,9},{11,1... | collective-permute-start | bytes 4718600 | tf_op jit(solution)/shard_map/ppermute | solution.py:25
  54.1 207.8 %copy-start.6 = (bf16[768,1024]{1,0:T(8,128)(2,1)}, bf16[768,1024]{1,0:T(8,128)(2,1)S(1)}, u32[]{:S(2)}) copy-start(bf16[768,1024]{1,0:T(8,128)(2,1)S(1)} %collective-permute-done.1) | copy-start | bytes 4718596
  54.1 22.7 %collective-permute-start.2 = (bf16[768,1024]{1,0:T(8,128)(2,1)S(1)}, bf16[768,1024]{1,0:T(8,128)(2,1)}, u32[]{:S(2)}, u32[]{:S(2)}) collective-permute-start(bf16[768,1024]{1,0:T(8,128)(2,1)S(1)} %collective-permute-done.1), channel_id=1, source_target_pairs={{0,1},{1,2},{2,3},{3,4},{4,5},{5,6},{6,7},{7,8},{8,9},{9,10},{10,1... | collective-permute-start | bytes 4718600 | tf_op jit(solution)/shard_map/ppermute | solution.py:23
  66.8 497.5 %reduce-scatter.3.cloned.1.call-start = ((), (), s32[]{:S(2)}) async-start(), calls=%async_computation.3 | async-start | bytes 4456448 | tf_op jit(solution)/shard_map/reduce_scatter | solution.py:82
  66.8 195.1 %copy-start.4 = (bf16[768,1024]{1,0:T(8,128)(2,1)}, bf16[768,1024]{1,0:T(8,128)(2,1)S(1)}, u32[]{:S(2)}) copy-start(bf16[768,1024]{1,0:T(8,128)(2,1)S(1)} %collective-permute-done.8) | copy-start | bytes 4718596
  66.9 37.7 %collective-permute-start.9 = (bf16[768,1024]{1,0:T(8,128)(2,1)S(1)}, bf16[768,1024]{1,0:T(8,128)(2,1)S(1)}, u32[]{:S(2)}, u32[]{:S(2)}) collective-permute-start(bf16[768,1024]{1,0:T(8,128)(2,1)S(1)} %collective-permute-done.8), channel_id=1, source_target_pairs={{1,0},{2,1},{3,2},{4,3},{5,4},{6,5},{7,6},{8,7},{9,8},{10,9},{11,1... | collective-permute-start | bytes 4718600 | tf_op jit(solution)/shard_map/ppermute | solution.py:25
  76.9 34.5 %collective-permute-start.3 = (bf16[768,1024]{1,0:T(8,128)(2,1)}, bf16[768,1024]{1,0:T(8,128)(2,1)S(1)}, u32[]{:S(2)}, u32[]{:S(2)}) collective-permute-start(bf16[768,1024]{1,0:T(8,128)(2,1)} %collective-permute-done.2), channel_id=1, source_target_pairs={{0,1},{1,2},{2,3},{3,4},{4,5},{5,6},{6,7},{7,8},{8,9},{9,10},{10,1... | collective-permute-start | bytes 4718600 | tf_op jit(solution)/shard_map/ppermute | solution.py:23
  105.7 47.2 %collective-permute-start.10 = (bf16[768,1024]{1,0:T(8,128)(2,1)S(1)}, bf16[768,1024]{1,0:T(8,128)(2,1)S(1)}, u32[]{:S(2)}, u32[]{:S(2)}) collective-permute-start(bf16[768,1024]{1,0:T(8,128)(2,1)S(1)} %collective-permute-done.9), channel_id=1, source_target_pairs={{1,0},{2,1},{3,2},{4,3},{5,4},{6,5},{7,6},{8,7},{9,8},{10,9},{11,1... | collective-permute-start | bytes 4718600 | tf_op jit(solution)/shard_map/ppermute | solution.py:25
  111.3 114.9 %copy-start.14 = (bf16[768,1024]{1,0:T(8,128)(2,1)}, bf16[768,1024]{1,0:T(8,128)(2,1)S(1)}, u32[]{:S(2)}) copy-start(bf16[768,1024]{1,0:T(8,128)(2,1)S(1)} %collective-permute-done.3) | copy-start | bytes 4718596
  111.3 52.5 %collective-permute-start.4 = (bf16[768,1024]{1,0:T(8,128)(2,1)S(1)}, bf16[768,1024]{1,0:T(8,128)(2,1)S(1)}, u32[]{:S(2)}, u32[]{:S(2)}) collective-permute-start(bf16[768,1024]{1,0:T(8,128)(2,1)S(1)} %collective-permute-done.3), channel_id=1, source_target_pairs={{0,1},{1,2},{2,3},{3,4},{4,5},{5,6},{6,7},{7,8},{8,9},{9,10},{10,1... | collective-permute-start | bytes 4718600 | tf_op jit(solution)/shard_map/ppermute | solution.py:23
  154.1 35.5 %collective-permute-start.11 = (bf16[768,1024]{1,0:T(8,128)(2,1)S(1)}, bf16[768,1024]{1,0:T(8,128)(2,1)S(1)}, u32[]{:S(2)}, u32[]{:S(2)}) collective-permute-start(bf16[768,1024]{1,0:T(8,128)(2,1)S(1)} %collective-permute-done.10), channel_id=1, source_target_pairs={{1,0},{2,1},{3,2},{4,3},{5,4},{6,5},{7,6},{8,7},{9,8},{10,9},{11,1... | collective-permute-start | bytes 4718600 | tf_op jit(solution)/shard_map/ppermute | solution.py:25
  163.8 62.4 %copy-start.16 = (bf16[768,1024]{1,0:T(8,128)(2,1)}, bf16[768,1024]{1,0:T(8,128)(2,1)S(1)}, u32[]{:S(2)}) copy-start(bf16[768,1024]{1,0:T(8,128)(2,1)S(1)} %collective-permute-done.4) | copy-start | bytes 4718596
  163.8 28.8 %collective-permute-start.5 = (bf16[768,1024]{1,0:T(8,128)(2,1)S(1)}, bf16[768,1024]{1,0:T(8,128)(2,1)S(1)}, u32[]{:S(2)}, u32[]{:S(2)}) collective-permute-start(bf16[768,1024]{1,0:T(8,128)(2,1)S(1)} %collective-permute-done.4), channel_id=1, source_target_pairs={{0,1},{1,2},{2,3},{3,4},{4,5},{5,6},{6,7},{7,8},{8,9},{9,10},{10,1... | collective-permute-start | bytes 4718600 | tf_op jit(solution)/shard_map/ppermute | solution.py:23
  190.7 35.5 %collective-permute-start.12 = (bf16[768,1024]{1,0:T(8,128)(2,1)S(1)}, bf16[768,1024]{1,0:T(8,128)(2,1)}, u32[]{:S(2)}, u32[]{:S(2)}) collective-permute-start(bf16[768,1024]{1,0:T(8,128)(2,1)S(1)} %collective-permute-done.11), channel_id=1, source_target_pairs={{1,0},{2,1},{3,2},{4,3},{5,4},{6,5},{7,6},{8,7},{9,8},{10,9},{11,1... | collective-permute-start | bytes 4718600 | tf_op jit(solution)/shard_map/ppermute | solution.py:25
  192.6 36.8 %copy-start.18 = (bf16[768,1024]{1,0:T(8,128)(2,1)}, bf16[768,1024]{1,0:T(8,128)(2,1)S(1)}, u32[]{:S(2)}) copy-start(bf16[768,1024]{1,0:T(8,128)(2,1)S(1)} %collective-permute-done.5) | copy-start | bytes 4718596
  192.6 36.8 %collective-permute-start.6 = (bf16[768,1024]{1,0:T(8,128)(2,1)S(1)}, bf16[768,1024]{1,0:T(8,128)(2,1)}, u32[]{:S(2)}, u32[]{:S(2)}) collective-permute-start(bf16[768,1024]{1,0:T(8,128)(2,1)S(1)} %collective-permute-done.5), channel_id=1, source_target_pairs={{0,1},{1,2},{2,3},{3,4},{4,5},{5,6},{6,7},{7,8},{8,9},{9,10},{10,1... | collective-permute-start | bytes 4718600 | tf_op jit(solution)/shard_map/ppermute | solution.py:23
  226.2 46.9 %collective-permute-start.13 = (bf16[768,1024]{1,0:T(8,128)(2,1)}, bf16[768,1024]{1,0:T(8,128)(2,1)}, u32[]{:S(2)}, u32[]{:S(2)}) collective-permute-start(bf16[768,1024]{1,0:T(8,128)(2,1)} %collective-permute-done.12), channel_id=1, source_target_pairs={{1,0},{2,1},{3,2},{4,3},{5,4},{6,5},{7,6},{8,7},{9,8},{10,9},{11,1... | collective-permute-start | bytes 4718600 | tf_op jit(solution)/shard_map/ppermute | solution.py:25
  229.4 44.0 %collective-permute-start.7 = (bf16[768,1024]{1,0:T(8,128)(2,1)}, bf16[768,1024]{1,0:T(8,128)(2,1)}, u32[]{:S(2)}, u32[]{:S(2)}) collective-permute-start(bf16[768,1024]{1,0:T(8,128)(2,1)} %collective-permute-done.6), channel_id=1, source_target_pairs={{0,1},{1,2},{2,3},{3,4},{4,5},{5,6},{6,7},{7,8},{8,9},{9,10},{10,1... | collective-permute-start | bytes 4718600 | tf_op jit(solution)/shard_map/ppermute | solution.py:23
  273.1 6.0 %copy-start.19 = (bf16[768,1024]{1,0:T(8,128)(2,1)S(1)}, bf16[768,1024]{1,0:T(8,128)(2,1)}, u32[]{:S(2)}) copy-start(bf16[768,1024]{1,0:T(8,128)(2,1)} %copy-done.18) | copy-start | bytes 4718596
  273.1 7.2 %copy-start.17 = (bf16[768,1024]{1,0:T(8,128)(2,1)S(1)}, bf16[768,1024]{1,0:T(8,128)(2,1)}, u32[]{:S(2)}) copy-start(bf16[768,1024]{1,0:T(8,128)(2,1)} %copy-done.16) | copy-start | bytes 4718596
  273.1 27.1 %collective-permute-start.14 = (bf16[768,1024]{1,0:T(8,128)(2,1)}, bf16[768,1024]{1,0:T(8,128)(2,1)S(1)}, u32[]{:S(2)}, u32[]{:S(2)}) collective-permute-start(bf16[768,1024]{1,0:T(8,128)(2,1)} %collective-permute-done.13), channel_id=1, source_target_pairs={{1,0},{2,1},{3,2},{4,3},{5,4},{6,5},{7,6},{8,7},{9,8},{10,9},{11,1... | collective-permute-start | bytes 4718600 | tf_op jit(solution)/shard_map/ppermute | solution.py:25
  276.2 5.4 copy-start.15
  280.4 5.4 copy-start.7
  281.7 5.3 copy-start.3
  282.9 5.4 copy-start.1
  287.0 3.9 copy-start.9
  289.6 4.0 copy-start.13
  464.7 115.6 %reduce-scatter.5.cloned.1.call-start = ((), (), s32[]{:S(2)}) async-start(), calls=%async_computation.4 | async-start | bytes 786432 | tf_op jit(solution)/shard_map/reduce_scatter | solution.py:91
  (6 other events, 12.3 us)
Sparse Core Ops, SparseCore 0:
  66.9 77.5 all-gather.1
  464.8 99.4 reduce-scatter.2
  566.5 13.6 reduce-scatter.4
